TPU v7x, 32 devices: a whole 2x2x4 slice. The times are simulated.
32 devices in a mesh: dp: 2 (over y), seq: 16 (over z, x, core).
Axes of the slice: x: 2, y: 2, z: 4, core: 2. Of those that a mesh axis runs over, the one named last changes fastest.
Arguments:
- q_img: bfloat16 [2, 2048, 2048], P('dp', 'seq'), may hold values from -6 to 6
- k_img: bfloat16 [2, 2048, 2048], P('dp', 'seq'), may hold values from -6 to 6
- v_img: bfloat16 [2, 2048, 2048], P('dp', 'seq'), may hold values from -12 to 12
- x_txt: bfloat16 [2, 77, 2432], P('dp'), may hold values from -9 to 9
- w_txt: bfloat16 [3, 2432, 2048], P(None, 'dp', 'seq'), may hold values from -0.125 to 0.125
- grad_img: bfloat16 [2, 2048, 2048], P('dp', 'seq'), may hold values from -6 to 6
- grad_txt: bfloat16 [2, 77, 2048], P('dp', None, 'seq'), may hold values from -6 to 6
Outputs:
- o_img: bfloat16 [2, 2048, 2048], P('dp', 'seq')
- o_txt: bfloat16 [2, 77, 2048], P('dp', None, 'seq')
- grad_qkv_img: bfloat16 [3, 2, 2048, 2048], P(None, 'dp', 'seq')
- dx_txt: float32 [2, 77, 2432], P('dp', None, 'seq')
- dw_txt: float32 [3, 2432, 2048], P(None, 'dp', 'seq')
All inputs are finite; a program needn't handle non-finite values.
Results may differ from a plain program's by a relative error of at most 0.014.
Values may be sent and summed in bfloat16 or wider, within the bound.
A program may use at most 64 MiB of HBM per device.

v0:
```python
import functools
import math

import jax
import jax.numpy as jnp
from jax import lax
from jax.experimental import pallas as pl
from jax.experimental.pallas import tpu as pltpu
from jax.sharding import PartitionSpec as P

HEAD_DIM = 64
BF = jnp.bfloat16
F32 = jnp.float32
NT = (((1,), (1,)), ((), ()))
TN = (((0,), (0,)), ((), ()))


def up(value, step):
    return (value + step - 1) // step * step


def dotf(a, b, dims=(((1,), (0,)), ((), ()))):
    return lax.dot_general(a, b, dims, preferred_element_type=F32)


def kernel(
    cfg,
    q_in, k_in, v_in, g_in, x_in, w_ref, gt_ref,
    o_out, gr_out, ot_out, dx_out, dw_out,
    kbuf, vbuf, qbuf, gbuf, xall, part, partl, kaug, kh, vaug, vh, pbuf, sbuf, gst, qst,
    obuf, dqbuf, dkacc, dvacc, dkb, dvb, tg, tgl, dxs, dxl,
    in_send, in_recv, out_send, out_recv, xs_sem, xr_sem, ps_sem, pr_sem, ts_sem, tr_sem,
    ds_sem, dr_sem, loc_sem,
):
    n, ndp, rows, cols, txt, tsub, tkey, dloc, dblk, group = cfg
    heads = cols // HEAD_DIM
    img = n * rows
    length = img + tkey
    m = group * rows
    steps = n // group
    nb = dloc // dblk
    me = lax.axis_index("seq")
    dp = lax.axis_index("dp")
    wide = cols % 128 == 0

    def tile(ref, j):
        if wide:
            return ref.at[:, pl.ds(pl.multiple_of(j * cols, 128), cols)]
        return ref.at[j]

    def at_rows(ref, j):
        return ref.at[pl.ds(pl.multiple_of(j * rows, 16), rows), :]

    barrier = pltpu.get_barrier_semaphore()
    total = n * ndp

    def greet(i, c):
        flat = lax.rem(dp * n + me + i, total)
        pl.semaphore_signal(
            barrier, inc=1, device_id={"dp": flat // n, "seq": lax.rem(flat, n)},
            device_id_type=pl.DeviceIdType.MESH,
        )
        return c

    lax.fori_loop(1, total, greet, 0)
    pl.semaphore_wait(barrier, total - 1)

    ins = (k_in, v_in, q_in, g_in)
    bufs = (kbuf, vbuf, qbuf, gbuf)

    def in_copy(a, dest, source):
        return pltpu.make_async_remote_copy(
            src_ref=tile(ins[a], dest), dst_ref=at_rows(bufs[a], source),
            send_sem=in_send.at[a, dest], recv_sem=in_recv.at[a, source],
            device_id={"seq": dest}, device_id_type=pl.DeviceIdType.MESH,
        )

    def own_copy(a):
        return pltpu.make_async_copy(tile(ins[a], me), at_rows(bufs[a], me), loc_sem.at[a])

    def x_copy(p, source):
        return pltpu.make_async_remote_copy(
            src_ref=x_in.at[p], dst_ref=xall.at[source],
            send_sem=xs_sem.at[p], recv_sem=xr_sem.at[source],
            device_id={"dp": p}, device_id_type=pl.DeviceIdType.MESH,
        )

    def p_copy(p, source):
        return pltpu.make_async_remote_copy(
            src_ref=part.at[p], dst_ref=partl.at[source],
            send_sem=ps_sem.at[p], recv_sem=pr_sem.at[source],
            device_id={"dp": p}, device_id_type=pl.DeviceIdType.MESH,
        )

    def t_copy(p, source):
        return pltpu.make_async_remote_copy(
            src_ref=tg, dst_ref=tgl.at[source],
            send_sem=ts_sem.at[p], recv_sem=tr_sem.at[source],
            device_id={"dp": p}, device_id_type=pl.DeviceIdType.MESH,
        )

    own_x = pltpu.make_async_copy(x_in.at[dp], xall.at[dp], loc_sem.at[4])
    own_x.start()
    for i in range(1, ndp):
        x_copy(lax.rem(dp + i, ndp), dp).start()

    def send_kv(i, c):
        dest = lax.rem(me + i, n)
        in_copy(0, dest, me).start()
        in_copy(1, dest, me).start()
        return c

    lax.fori_loop(1, n, send_kv, 0)
    for a in range(4):
        own_copy(a).start()
    my_group = me // group

    def send_qg(t, c):
        for e in range(group):
            dest = lax.rem(my_group + steps - t, steps) * group + e

            @pl.when(dest != me)
            def _():
                in_copy(2, dest, me).start()
                in_copy(3, dest, me).start()

        return c

    lax.fori_loop(0, steps, send_qg, 0)

    own_x.wait()
    for i in range(ndp):
        s = lax.rem(dp + i, ndp)
        if i:
            x_copy(dp, s).wait_recv()
        for j in range(3):
            product = dotf(xall[s], w_ref[j])
            if i:
                part[s, j] = product
            else:
                partl[dp, j] = product
        if i:
            p_copy(s, dp).start()
    for i in range(1, ndp):
        p_copy(dp, lax.rem(dp + i, ndp)).wait_recv()
    for j, buf in enumerate((qbuf, kbuf, vbuf)):
        value = partl[0, j]
        for s in range(1, ndp):
            value = value + partl[s, j]
        buf[pl.ds(img, tsub), :] = value.astype(BF)
        pad = buf.shape[0] - img - tsub
        buf[pl.ds(img + tsub, pad), :] = jnp.zeros((pad, cols), BF)
    gbuf[pl.ds(img, tsub), :] = gt_ref[...]
    pad = gbuf.shape[0] - img - tsub
    gbuf[pl.ds(img + tsub, pad), :] = jnp.zeros((pad, cols), BF)
    dkacc[...] = jnp.zeros_like(dkacc)
    dvacc[...] = jnp.zeros_like(dvacc)

    def wait_kv(i, c):
        source = lax.rem(me + i, n)
        in_copy(0, me, source).wait_recv()
        in_copy(1, me, source).wait_recv()
        return c

    lax.fori_loop(1, n, wait_kv, 0)
    for a in range(4):
        own_copy(a).wait()

    lane_head = lax.broadcasted_iota(jnp.int32, (m, cols), 1) // HEAD_DIM

    def build(r, c):
        at = pl.ds(pl.multiple_of(r * 128, 128), 128)
        lane = lax.broadcasted_iota(jnp.int32, (128, cols), 1)
        row = lax.broadcasted_iota(jnp.int32, (128, cols), 0) + r * 128
        kk = kbuf[at, :]
        vv = vbuf[at, :]
        bias = jnp.where((row >= img + txt) & (lane == 0), -1e30, 0.0).astype(BF)
        ones = jnp.ones((128, cols), BF)
        zero = jnp.zeros((128, cols), BF)
        kaug[at, :] = jnp.concatenate([kk, bias], axis=1)
        vaug[at, :] = jnp.concatenate([vv, ones], axis=1)
        for h in range(heads):
            mine = lane // HEAD_DIM == h
            kh[h, at, :] = jnp.where(mine, kk, zero)
            vh[h, at, :] = jnp.concatenate(
                [jnp.where(mine, vv, zero), jnp.where(mine, ones, zero)], axis=1
            )
        return c

    lax.fori_loop(0, length // 128, build, 0)
    scale = 1.0 / math.sqrt(HEAD_DIM)

    def out_copy(a, dest, source):
        send = (obuf, dqbuf, dkb, dvb)[a]
        land = o_out if a == 0 else gr_out.at[a - 1]
        return pltpu.make_async_remote_copy(
            src_ref=at_rows(send, dest), dst_ref=tile(land, source),
            send_sem=out_send.at[a, dest], recv_sem=out_recv.at[a, source],
            device_id={"seq": dest}, device_id_type=pl.DeviceIdType.MESH,
        )

    def own_out(a):
        send = (obuf, dqbuf, dkb, dvb)[a]
        land = o_out if a == 0 else gr_out.at[a - 1]
        return pltpu.make_async_copy(at_rows(send, me), tile(land, me), loc_sem.at[5 + a])

    def step(t, c):
        which = lax.rem(my_group + t + steps - 1, steps)
        first = jnp.where(t == 0, img, which * m)
        for e in range(group):
            source = which * group + e

            @pl.when((t > 0) & (source != me))
            def _():
                in_copy(2, me, source).wait_recv()
                in_copy(3, me, source).wait_recv()

        at = pl.ds(pl.multiple_of(first, 128), m)
        qs = qbuf[at, :] * jnp.asarray(scale, BF)
        g = gbuf[at, :].astype(F32)
        zero = jnp.zeros_like(qs)
        one = jnp.where(lax.broadcasted_iota(jnp.int32, (m, cols), 1) == 0, 1.0, 0.0).astype(BF)
        acc = jnp.zeros((m, 2 * cols), F32)
        for h in range(heads):
            qm = jnp.where(lane_head == h, qs, zero)
            qst[pl.ds(h * m, m), :] = qm
            scores = dotf(jnp.concatenate([qm, one], axis=1), kaug[...], NT)
            top = jnp.max(scores, axis=1, keepdims=True)
            p = jnp.exp(scores - top).astype(BF)
            pbuf[pl.ds(h * m, m), :] = p
            acc = acc + dotf(p, vh[h])
        inverse = 1.0 / acc[:, cols:]
        ob = (acc[:, :cols] * inverse).astype(BF)
        gp = (g * inverse).astype(BF)
        term = -(ob.astype(F32) * gp.astype(F32)).astype(BF)
        dq = jnp.zeros((m, cols), F32)
        for h in range(heads):
            gm = jnp.where(lane_head == h, gp, zero)
            gst[pl.ds(h * m, m), :] = gm
            lhs = jnp.concatenate([gm, jnp.where(lane_head == h, term, zero)], axis=1)
            inner = dotf(lhs, vaug[...], NT)
            ds = inner.astype(BF) * pbuf[pl.ds(h * m, m), :]
            sbuf[pl.ds(h * m, m), :] = ds
            dq = dq + dotf(ds, kh[h])
        obuf[at, :] = ob
        dqbuf[at, :] = (dq * scale).astype(BF)
        for e in range(group):
            dest = which * group + e

            @pl.when((t > 0) & (dest != me))
            def _():
                out_copy(0, dest, me).start()
                out_copy(1, dest, me).start()

            @pl.when((t > 0) & (dest == me))
            def _():
                own_out(0).start()
                own_out(1).start()

        dvacc[...] += dotf(pbuf[...], gst[...], TN)
        dkacc[...] += dotf(sbuf[...], qst[...], TN)
        return c

    lax.fori_loop(0, steps + 1, step, 0)

    text = pl.ds(img, tsub)
    tg[0] = dqbuf[text, :]
    tg[1] = dkacc[text, :].astype(BF)
    tg[2] = dvacc[text, :].astype(BF)
    for i in range(1, ndp):
        t_copy(lax.rem(dp + i, ndp), dp).start()
    ot_out[...] = obuf[text, :]

    def send_dkv(i, c):
        dest = lax.rem(me + i, n)
        at = pl.ds(pl.multiple_of(dest * rows, 16), rows)
        dkb[at, :] = dkacc[at, :].astype(BF)
        dvb[at, :] = dvacc[at, :].astype(BF)

        @pl.when(dest != me)
        def _():
            out_copy(2, dest, me).start()
            out_copy(3, dest, me).start()

        @pl.when(dest == me)
        def _():
            own_out(2).start()
            own_out(3).start()

        return c

    lax.fori_loop(1, n + 1, send_dkv, 0)

    tgl[dp] = tg[...]
    for i in range(1, ndp):
        t_copy(dp, lax.rem(dp + i, ndp)).wait_recv()

    def dx_copy(s, b, source):
        return pltpu.make_async_remote_copy(
            src_ref=dxs.at[s, b], dst_ref=dxl.at[source],
            send_sem=ds_sem.at[s, b], recv_sem=dr_sem.at[source],
            device_id={"dp": s, "seq": dp * nb + b}, device_id_type=pl.DeviceIdType.MESH,
        )

    for s in range(ndp):
        value = dotf(tgl[s, 0], w_ref[0], NT)
        for j in range(1, 3):
            value = value + dotf(tgl[s, j], w_ref[j], NT)
        for b in range(nb):
            dxs[s, b] = value[:, b * dblk:(b + 1) * dblk].astype(BF)
        for b in range(nb):
            mine = (dp == s) & (dp * nb + b == me)

            @pl.when(jnp.logical_not(mine))
            def _():
                dx_copy(s, b, me).start()

            @pl.when(mine)
            def _():
                pltpu.make_async_copy(dxs.at[s, b], dxl.at[me], dr_sem.at[me]).start()

    for j in range(3):
        value = dotf(xall[0], tgl[0, j], TN)
        for s in range(1, ndp):
            value = value + dotf(xall[s], tgl[s, j], TN)
        dw_out[j] = value

    holder = me // nb
    own_dx = holder == dp

    def wait_dx(r, c):
        @pl.when(jnp.logical_not(own_dx & (r == me)))
        def _():
            dx_copy(0, 0, r).wait_recv()

        @pl.when(own_dx & (r == me))
        def _():
            pltpu.make_async_copy(dxs.at[0, 0], dxl.at[r], dr_sem.at[r]).wait()

        return c

    lax.fori_loop(0, n, wait_dx, 0)
    sums = dxl[0].astype(F32)
    for r in range(1, n):
        sums = sums + dxl[r].astype(F32)
    dx_out[...] = sums

    for a in range(4):
        own_out(a).wait()

    def drain(i, c):
        other = lax.rem(me + i, n)
        for a in range(4):
            out_copy(a, me, other).wait_recv()
            out_copy(a, other, me).wait_send()
            in_copy(a, other, me).wait_send()
        return c

    lax.fori_loop(1, n, drain, 0)
    for i in range(1, ndp):
        p = lax.rem(dp + i, ndp)
        x_copy(p, dp).wait_send()
        p_copy(p, dp).wait_send()
        t_copy(p, dp).wait_send()
    for s in range(ndp):
        for b in range(nb):

            @pl.when(jnp.logical_not((dp == s) & (dp * nb + b == me)))
            def _():
                dx_copy(s, b, me).wait_send()


def local(n, ndp, q_img, k_img, v_img, x_txt, w_txt, grad_img, grad_txt):
    _, rows, hd = q_img.shape
    cols = hd // n
    heads = cols // HEAD_DIM
    txt, width = x_txt.shape[1:]
    dloc = w_txt.shape[1]
    dblk = width // n
    tsub = up(txt, 16)
    tkey = up(txt, 128)
    group = 2
    m = group * rows
    nb = dloc // dblk
    length = n * rows + tkey
    qlen = n * rows + m
    wide = cols % 128 == 0

    def spread(a):
        return a[0] if wide else a[0].reshape(rows, n, cols).transpose(1, 0, 2)

    x_parts = jnp.pad(x_txt[0], ((0, tsub - txt), (0, 0)))
    x_parts = x_parts.reshape(tsub, ndp, dloc).transpose(1, 0, 2)
    gt = jnp.pad(grad_txt[0], ((0, tsub - txt), (0, 0)))
    shape = (rows, hd) if wide else (n, rows, cols)
    hbm = pl.BlockSpec(memory_space=pl.ANY)
    vmem = pl.BlockSpec(memory_space=pltpu.VMEM)
    cfg = (n, ndp, rows, cols, txt, tsub, tkey, dloc, dblk, group)
    dma = pltpu.SemaphoreType.DMA
    o, gr, ot, dx, dw = pl.pallas_call(
        functools.partial(kernel, cfg),
        out_shape=(
            jax.ShapeDtypeStruct(shape, BF),
            jax.ShapeDtypeStruct((3,) + shape, BF),
            jax.ShapeDtypeStruct((tsub, cols), BF),
            jax.ShapeDtypeStruct((tsub, dblk), F32),
            jax.ShapeDtypeStruct((3, dloc, cols), F32),
        ),
        in_specs=[hbm] * 5 + [vmem] * 2,
        out_specs=(hbm, hbm, vmem, vmem, vmem),
        scratch_shapes=[
            pltpu.VMEM((length, cols), BF),
            pltpu.VMEM((length, cols), BF),
            pltpu.VMEM((qlen, cols), BF),
            pltpu.VMEM((qlen, cols), BF),
            pltpu.VMEM((ndp, tsub, dloc), BF),
            pltpu.VMEM((ndp, 3, tsub, cols), F32),
            pltpu.VMEM((ndp, 3, tsub, cols), F32),
            pltpu.VMEM((length, 2 * cols), BF),
            pltpu.VMEM((heads, length, cols), BF),
            pltpu.VMEM((length, 2 * cols), BF),
            pltpu.VMEM((heads, length, 2 * cols), BF),
            pltpu.VMEM((heads * m, length), BF),
            pltpu.VMEM((heads * m, length), BF),
            pltpu.VMEM((heads * m, cols), BF),
            pltpu.VMEM((heads * m, cols), BF),
            pltpu.VMEM((qlen, cols), BF),
            pltpu.VMEM((qlen, cols), BF),
            pltpu.VMEM((length, cols), F32),
            pltpu.VMEM((length, cols), F32),
            pltpu.VMEM((length, cols), BF),
            pltpu.VMEM((length, cols), BF),
            pltpu.VMEM((3, tsub, cols), BF),
            pltpu.VMEM((ndp, 3, tsub, cols), BF),
            pltpu.VMEM((ndp, nb, tsub, dblk), BF),
            pltpu.VMEM((n, tsub, dblk), BF),
            dma((4, n)), dma((4, n)), dma((4, n)), dma((4, n)),
            dma((ndp,)), dma((ndp,)), dma((ndp,)), dma((ndp,)), dma((ndp,)), dma((ndp,)),
            dma((ndp, nb)), dma((n,)), dma((9,)),
        ],
        compiler_params=pltpu.CompilerParams(
            collective_id=0, has_side_effects=True, vmem_limit_bytes=60 * 1024 * 1024
        ),
    )(spread(q_img), spread(k_img), spread(v_img), spread(grad_img), x_parts, w_txt, gt)
    if not wide:
        o = o.transpose(1, 0, 2).reshape(rows, hd)
        gr = gr.transpose(0, 2, 1, 3).reshape(3, rows, hd)
    return (o[None], ot[None, :txt], gr[:, None], dx[None, :txt], dw)


def solution(mesh):
    n, ndp = mesh.shape["seq"], mesh.shape["dp"]
    in_specs = (
        P("dp", "seq", None),
        P("dp", "seq", None),
        P("dp", "seq", None),
        P("dp", None, None),
        P(None, "dp", "seq"),
        P("dp", "seq", None),
        P("dp", None, "seq"),
    )
    out_specs = (
        P("dp", "seq", None),
        P("dp", None, "seq"),
        P(None, "dp", "seq", None),
        P("dp", None, "seq"),
        P(None, "dp", "seq"),
    )
    return jax.shard_map(
        functools.partial(local, n, ndp), mesh=mesh, in_specs=in_specs, out_specs=out_specs,
        check_vma=False,
    )
```

profile of v0, /device:TPU:31, one launch (start us, length us, event | category | flops | bytes accessed | tf_op | source)
XLA Modules:
  0.0 151.4 jit_solution(7205146472848508355)
XLA Ops:
  0.6 1.3 pad.9.gt_ref
  2.0 1.0 pad.8
  3.0 0.4 reshape.13
  3.4 0.8 copy.18
  4.2 138.3 %shard_map.110 = (bf16[128,2048]{1,0:T(8,128)(2,1)}, bf16[3,128,2048]{2,1,0:T(8,128)(2,1)}, bf16[80,128]{1,0:T(8,128)(2,1)}, f32[80,152]{1,0:T(8,128)}, f32[3,1216,128]{2,1,0:T(8,128)}) custom-call(bf16[128,2048]{1,0:T(8,128)(2,1)} %bitcast.20, bf16[128,2048]{1,0:T(8,128)(2,1)} %bitcast.21, bf16[128,2048]{1,0:T(8,128)(2,1)} %bitcast.22, ...), custom_call_target="tpu_custom_call" | custom-call | tf_op jit(solution)/shard_map/pallas_call | solution.py:400
  142.5 1.3 slice_bitcast_fusion.1
  143.8 0.9 slice_bitcast_fusion
  144.7 0.7 copy.16
  145.5 0.0 copy-start
  145.5 2.0 %copy.22 = bf16[1,128,2048]{2,1,0:T(8,128)(2,1)} copy(bf16[1,128,2048]{2,1,0:T(8,128)(2,1)} %bitcast.19) | data formatting | bytes 1048576
  147.5 2.7 %copy.23 = bf16[3,1,128,2048]{3,2,1,0:T(8,128)(2,1)} copy(bf16[3,1,128,2048]{3,2,1,0:T(8,128)(2,1)} %bitcast.18) | data formatting | bytes 3145728
  150.2 0.0 copy-done
  150.2 1.2 copy.24
Async XLA Ops:
  145.5 4.7 %copy-start = (f32[3,1216,128]{2,1,0:T(8,128)S(1)}, f32[3,1216,128]{2,1,0:T(8,128)}, u32[]{:S(2)}) copy-start(f32[3,1216,128]{2,1,0:T(8,128)} %get-tuple-element.34) | copy-start | bytes 5603332
where the time goes:
time: 152 us; the launch traced here: 151 us
  Pallas kernels  138 us (91%)
  local copies, waits for them, and re-layouts  12.5 us (8%)
    pallas_call x1, Pallas kernels, local(): pl.pallas_call(functools.partial(kernel, cfg), out_shape=(jax.ShapeDtypeS...  138 us
    unnamed x6, local copies, waits for them, and re-layouts  6.72 us

commit v1 on v0

--- a/solution.py
+++ b/solution.py
@@ -9,6 +9,7 @@
 from jax.sharding import PartitionSpec as P
 
 HEAD_DIM = 64
+QUAD = 4
 BF = jnp.bfloat16
 F32 = jnp.float32
 NT = (((1,), (1,)), ((), ()))
@@ -25,12 +26,13 @@
 
 def kernel(
     cfg,
-    q_in, k_in, v_in, g_in, x_in, w_ref, gt_ref,
-    o_out, gr_out, ot_out, dx_out, dw_out,
+    q_in, k_in, v_in, g_in, x_ref, w_ref, gt_ref,
+    o_out, gr_out, ot_out, dx_out, x_out, tg_out,
     kbuf, vbuf, qbuf, gbuf, xall, part, partl, kaug, kh, vaug, vh, pbuf, sbuf, gst, qst,
-    obuf, dqbuf, dkacc, dvacc, dkb, dvb, tg, tgl, dxs, dxl,
+    obuf, dqbuf, dkacc, dvacc, dkb, dvb, tg, tgl, dxs, dx1, dx2, dxl,
+    xf, gf, xs,
     in_send, in_recv, out_send, out_recv, xs_sem, xr_sem, ps_sem, pr_sem, ts_sem, tr_sem,
-    ds_sem, dr_sem, loc_sem,
+    d1s_sem, d1r_sem, ds_sem, dr_sem, loc_sem,
 ):
     n, ndp, rows, cols, txt, tsub, tkey, dloc, dblk, group = cfg
     heads = cols // HEAD_DIM
@@ -80,7 +82,7 @@
 
     def x_copy(p, source):
         return pltpu.make_async_remote_copy(
-            src_ref=x_in.at[p], dst_ref=xall.at[source],
+            src_ref=xs.at[p], dst_ref=xall.at[source],
             send_sem=xs_sem.at[p], recv_sem=xr_sem.at[source],
             device_id={"dp": p}, device_id_type=pl.DeviceIdType.MESH,
         )
@@ -98,11 +100,6 @@
             send_sem=ts_sem.at[p], recv_sem=tr_sem.at[source],
             device_id={"dp": p}, device_id_type=pl.DeviceIdType.MESH,
         )
-
-    own_x = pltpu.make_async_copy(x_in.at[dp], xall.at[dp], loc_sem.at[4])
-    own_x.start()
-    for i in range(1, ndp):
-        x_copy(lax.rem(dp + i, ndp), dp).start()
 
     def send_kv(i, c):
         dest = lax.rem(me + i, n)
@@ -128,7 +125,17 @@
 
     lax.fori_loop(0, steps, send_qg, 0)
 
-    own_x.wait()
+    xf[...] = jnp.zeros_like(xf)
+    xf[pl.ds(0, txt), :] = x_ref[...].astype(F32)
+    whole_x = xf[...]
+    for p in range(ndp):
+        xs[p] = whole_x[:, p * dloc:(p + 1) * dloc].astype(BF)
+    for i in range(1, ndp):
+        x_copy(lax.rem(dp + i, ndp), dp).start()
+    xall[dp] = xs[dp]
+    gf[...] = jnp.zeros_like(gf)
+    gf[pl.ds(0, txt), :] = gt_ref[...].astype(F32)
+
     for i in range(ndp):
         s = lax.rem(dp + i, ndp)
         if i:
@@ -150,7 +157,7 @@
         buf[pl.ds(img, tsub), :] = value.astype(BF)
         pad = buf.shape[0] - img - tsub
         buf[pl.ds(img + tsub, pad), :] = jnp.zeros((pad, cols), BF)
-    gbuf[pl.ds(img, tsub), :] = gt_ref[...]
+    gbuf[pl.ds(img, tsub), :] = gf[...].astype(BF)
     pad = gbuf.shape[0] - img - tsub
     gbuf[pl.ds(img + tsub, pad), :] = jnp.zeros((pad, cols), BF)
     dkacc[...] = jnp.zeros_like(dkacc)
@@ -269,7 +276,7 @@
     tg[2] = dvacc[text, :].astype(BF)
     for i in range(1, ndp):
         t_copy(lax.rem(dp + i, ndp), dp).start()
-    ot_out[...] = obuf[text, :]
+    ot_out[...] = obuf[text, :].astype(F32)[:txt].astype(BF)
 
     def send_dkv(i, c):
         dest = lax.rem(me + i, n)
@@ -295,55 +302,74 @@
     for i in range(1, ndp):
         t_copy(dp, lax.rem(dp + i, ndp)).wait_recv()
 
-    def dx_copy(s, b, source):
-        return pltpu.make_async_remote_copy(
-            src_ref=dxs.at[s, b], dst_ref=dxl.at[source],
-            send_sem=ds_sem.at[s, b], recv_sem=dr_sem.at[source],
-            device_id={"dp": s, "seq": dp * nb + b}, device_id_type=pl.DeviceIdType.MESH,
-        )
+    part_of = lax.rem(me, QUAD)
+    base = me - part_of
+    slot = me // QUAD
+    per = nb // QUAD
+
+    def d1_copy(e, source):
+        return pltpu.make_async_remote_copy(
+            src_ref=dxs.at[e], dst_ref=dx1.at[source],
+            send_sem=d1s_sem.at[e], recv_sem=d1r_sem.at[source],
+            device_id={"seq": base + e}, device_id_type=pl.DeviceIdType.MESH,
+        )
+
+    def d2_copy(k, source):
+        owner = dp * nb + (k % per) * QUAD + part_of
+        return pltpu.make_async_remote_copy(
+            src_ref=dx2.at[k], dst_ref=dxl.at[source],
+            send_sem=ds_sem.at[k], recv_sem=dr_sem.at[source],
+            device_id={"dp": k // per, "seq": owner}, device_id_type=pl.DeviceIdType.MESH,
+        )
+
+    def d2_own(k):
+        return pltpu.make_async_copy(dx2.at[k], dxl.at[slot], dr_sem.at[slot])
+
+    def is_own(k):
+        return (dp == k // per) & (dp * nb + (k % per) * QUAD + part_of == me)
 
     for s in range(ndp):
-        value = dotf(tgl[s, 0], w_ref[0], NT)
+        value = dotf(w_ref[0], tgl[s, 0], NT)
         for j in range(1, 3):
-            value = value + dotf(tgl[s, j], w_ref[j], NT)
+            value = value + dotf(w_ref[j], tgl[s, j], NT)
         for b in range(nb):
-            dxs[s, b] = value[:, b * dblk:(b + 1) * dblk].astype(BF)
-        for b in range(nb):
-            mine = (dp == s) & (dp * nb + b == me)
-
-            @pl.when(jnp.logical_not(mine))
-            def _():
-                dx_copy(s, b, me).start()
-
-            @pl.when(mine)
-            def _():
-                pltpu.make_async_copy(dxs.at[s, b], dxl.at[me], dr_sem.at[me]).start()
-
-    for j in range(3):
-        value = dotf(xall[0], tgl[0, j], TN)
-        for s in range(1, ndp):
-            value = value + dotf(xall[s], tgl[s, j], TN)
-        dw_out[j] = value
-
-    holder = me // nb
-    own_dx = holder == dp
-
-    def wait_dx(r, c):
-        @pl.when(jnp.logical_not(own_dx & (r == me)))
-        def _():
-            dx_copy(0, 0, r).wait_recv()
-
-        @pl.when(own_dx & (r == me))
-        def _():
-            pltpu.make_async_copy(dxs.at[0, 0], dxl.at[r], dr_sem.at[r]).wait()
-
-        return c
-
-    lax.fori_loop(0, n, wait_dx, 0)
+            dxs[b % QUAD, s * per + b // QUAD] = value[b * dblk:(b + 1) * dblk, :].astype(BF)
+    for i in range(1, QUAD):
+        d1_copy(lax.rem(part_of + i, QUAD), part_of).start()
+    x_out[...] = xall[...]
+    tg_out[...] = tgl[...]
+    for i in range(1, QUAD):
+        d1_copy(part_of, lax.rem(part_of + i, QUAD)).wait_recv()
+    for k in range(ndp * per):
+        sums = dxs[part_of, k].astype(F32)
+        for i in range(1, QUAD):
+            sums = sums + dx1[lax.rem(part_of + i, QUAD), k].astype(F32)
+        dx2[k] = sums.astype(BF)
+    for k in range(ndp * per):
+
+        @pl.when(jnp.logical_not(is_own(k)))
+        def _():
+            d2_copy(k, slot).start()
+
+        @pl.when(is_own(k))
+        def _():
+            d2_own(k).start()
+
+    local_dx = me // nb == dp
+    for r in range(n // QUAD):
+
+        @pl.when(jnp.logical_not(local_dx & (slot == r)))
+        def _():
+            d2_copy(0, r).wait_recv()
+
+        @pl.when(local_dx & (slot == r))
+        def _():
+            d2_own(0).wait()
+
     sums = dxl[0].astype(F32)
-    for r in range(1, n):
+    for r in range(1, n // QUAD):
         sums = sums + dxl[r].astype(F32)
-    dx_out[...] = sums
+    dx_out[...] = sums[:, :txt]
 
     for a in range(4):
         own_out(a).wait()
@@ -362,12 +388,42 @@
         x_copy(p, dp).wait_send()
         p_copy(p, dp).wait_send()
         t_copy(p, dp).wait_send()
-    for s in range(ndp):
-        for b in range(nb):
-
-            @pl.when(jnp.logical_not((dp == s) & (dp * nb + b == me)))
-            def _():
-                dx_copy(s, b, me).wait_send()
+    for i in range(1, QUAD):
+        d1_copy(lax.rem(part_of + i, QUAD), part_of).wait_send()
+    for k in range(ndp * per):
+
+        @pl.when(jnp.logical_not(is_own(k)))
+        def _():
+            d2_copy(k, slot).wait_send()
+
+
+def finish(o_in, gr_in, ot_in, dx_in, x_ref, tg_ref, o_out, gr_out, ot_out, dx_out, dw_out, hold, dwb, in_sem, out_sem):
+    def fetch(i):
+        return pltpu.make_async_copy(o_in if i == 0 else gr_in.at[i - 1], hold.at[i], in_sem.at[i])
+
+    def put(i):
+        return pltpu.make_async_copy(hold.at[i], o_out if i == 0 else gr_out.at[i - 1], out_sem.at[i])
+
+    def put_dw(j):
+        return pltpu.make_async_copy(dwb.at[j], dw_out.at[j], out_sem.at[4 + j])
+
+    for i in range(4):
+        fetch(i).start()
+    ot_out[...] = ot_in[...]
+    dx_out[...] = dx_in[...]
+    for i in range(4):
+        fetch(i).wait()
+        put(i).start()
+        if i < 3:
+            value = dotf(x_ref[0], tg_ref[0, i], TN)
+            for s in range(1, x_ref.shape[0]):
+                value = value + dotf(x_ref[s], tg_ref[s, i], TN)
+            dwb[i] = value
+            put_dw(i).start()
+    for i in range(4):
+        put(i).wait()
+    for j in range(3):
+        put_dw(j).wait()
 
 
 def local(n, ndp, q_img, k_img, v_img, x_txt, w_txt, grad_img, grad_txt):
@@ -389,25 +445,24 @@
     def spread(a):
         return a[0] if wide else a[0].reshape(rows, n, cols).transpose(1, 0, 2)
 
-    x_parts = jnp.pad(x_txt[0], ((0, tsub - txt), (0, 0)))
-    x_parts = x_parts.reshape(tsub, ndp, dloc).transpose(1, 0, 2)
-    gt = jnp.pad(grad_txt[0], ((0, tsub - txt), (0, 0)))
     shape = (rows, hd) if wide else (n, rows, cols)
     hbm = pl.BlockSpec(memory_space=pl.ANY)
     vmem = pl.BlockSpec(memory_space=pltpu.VMEM)
     cfg = (n, ndp, rows, cols, txt, tsub, tkey, dloc, dblk, group)
     dma = pltpu.SemaphoreType.DMA
-    o, gr, ot, dx, dw = pl.pallas_call(
+    assert nb % QUAD == 0 and n % QUAD == 0
+    o, gr, ot, dx, xa, tga = pl.pallas_call(
         functools.partial(kernel, cfg),
         out_shape=(
             jax.ShapeDtypeStruct(shape, BF),
             jax.ShapeDtypeStruct((3,) + shape, BF),
-            jax.ShapeDtypeStruct((tsub, cols), BF),
-            jax.ShapeDtypeStruct((tsub, dblk), F32),
-            jax.ShapeDtypeStruct((3, dloc, cols), F32),
+            jax.ShapeDtypeStruct((txt, cols), BF),
+            jax.ShapeDtypeStruct((dblk, txt), F32),
+            jax.ShapeDtypeStruct((ndp, tsub, dloc), BF),
+            jax.ShapeDtypeStruct((ndp, 3, tsub, cols), BF),
         ),
-        in_specs=[hbm] * 5 + [vmem] * 2,
-        out_specs=(hbm, hbm, vmem, vmem, vmem),
+        in_specs=[hbm] * 4 + [vmem] * 3,
+        out_specs=(hbm, hbm, vmem, vmem, vmem, vmem),
         scratch_shapes=[
             pltpu.VMEM((length, cols), BF),
             pltpu.VMEM((length, cols), BF),
@@ -432,20 +487,40 @@
             pltpu.VMEM((length, cols), BF),
             pltpu.VMEM((3, tsub, cols), BF),
             pltpu.VMEM((ndp, 3, tsub, cols), BF),
-            pltpu.VMEM((ndp, nb, tsub, dblk), BF),
-            pltpu.VMEM((n, tsub, dblk), BF),
+            pltpu.VMEM((QUAD, ndp * nb // QUAD, dblk, tsub), BF),
+            pltpu.VMEM((QUAD, ndp * nb // QUAD, dblk, tsub), BF),
+            pltpu.VMEM((ndp * nb // QUAD, dblk, tsub), BF),
+            pltpu.VMEM((n // QUAD, dblk, tsub), BF),
+            pltpu.VMEM((tsub, width), F32),
+            pltpu.VMEM((tsub, cols), F32),
+            pltpu.VMEM((ndp, tsub, dloc), BF),
             dma((4, n)), dma((4, n)), dma((4, n)), dma((4, n)),
             dma((ndp,)), dma((ndp,)), dma((ndp,)), dma((ndp,)), dma((ndp,)), dma((ndp,)),
-            dma((ndp, nb)), dma((n,)), dma((9,)),
+            dma((QUAD,)), dma((QUAD,)), dma((ndp * nb // QUAD,)), dma((n // QUAD,)), dma((9,)),
         ],
         compiler_params=pltpu.CompilerParams(
             collective_id=0, has_side_effects=True, vmem_limit_bytes=60 * 1024 * 1024
         ),
-    )(spread(q_img), spread(k_img), spread(v_img), spread(grad_img), x_parts, w_txt, gt)
+    )(spread(q_img), spread(k_img), spread(v_img), spread(grad_img), x_txt[0], w_txt, grad_txt[0])
+    o, gr, ot, dx, dw = pl.pallas_call(
+        finish,
+        out_shape=(
+            jax.ShapeDtypeStruct(shape, BF),
+            jax.ShapeDtypeStruct((3,) + shape, BF),
+            jax.ShapeDtypeStruct((txt, cols), BF),
+            jax.ShapeDtypeStruct((dblk, txt), F32),
+            jax.ShapeDtypeStruct((3, dloc, cols), F32),
+        ),
+        in_specs=[hbm] * 2 + [vmem] * 4,
+        out_specs=(hbm, hbm, vmem, vmem, hbm),
+        scratch_shapes=[
+            pltpu.VMEM((4,) + shape, BF), pltpu.VMEM((3, dloc, cols), F32), dma((4,)), dma((7,)),
+        ],
+    )(o, gr, ot, dx, xa, tga)
     if not wide:
         o = o.transpose(1, 0, 2).reshape(rows, hd)
         gr = gr.transpose(0, 2, 1, 3).reshape(3, rows, hd)
-    return (o[None], ot[None, :txt], gr[:, None], dx[None, :txt], dw)
+    return (o[None], ot[None], gr[:, None], dx.T[None], dw)
 
 
 def solution(mesh):

time: 152 us -> 125 us (0.82)
  the two profiles are of different devices: /device:TPU:31 before, /device:TPU:7 now
where the time goes in v1:
time: 125 us
  Pallas kernels  124 us (99%)
    pallas_call x1, Pallas kernels, local(): pl.pallas_call(functools.partial(kernel, cfg), out_shape=(jax.ShapeDtypeS...  119 us
    pallas_call x1, Pallas kernels, local(): pl.pallas_call(finish, out_shape=(jax.ShapeDtypeStruct(shape, BF), jax.Sh...  5.23 us

profile of v1, /device:TPU:7, one launch (start us, length us, event | category | flops | bytes accessed | tf_op | source)
XLA Modules:
  0.0 125.1 jit_solution(8377984518082781209)
XLA Ops:
  0.6 119.2 %shard_map.110 = (bf16[128,2048]{1,0:T(8,128)(2,1)}, bf16[3,128,2048]{2,1,0:T(8,128)(2,1)}, bf16[77,128]{1,0:T(8,128)(2,1)}, f32[152,77]{1,0:T(8,128)}, bf16[2,8...) custom-call(bf16[128,2048]{1,0:T(8,128)(2,1)} %bitcast.14, bf16[128,2048]{1,0:T(8,128)(2,1)} %bitcast.15, ...), custom_call_target="tpu_custom_call" | custom-call | tf_op jit(solution)/shard_map/pallas_call | solution.py:454
  119.9 5.2 %shard_map.111 = (bf16[128,2048]{1,0:T(8,128)(2,1)}, bf16[3,128,2048]{2,1,0:T(8,128)(2,1)}, bf16[77,128]{1,0:T(8,128)(2,1)}, f32[152,77]{1,0:T(8,128)}, f32[3,1216,128]{2,1,0:T(8,128)}) custom-call(bf16[128,2048]{1,0:T(8,128)(2,1)} %get-tuple-element.16.o_in, bf16[3,128,2048]{2,1,0:T(8,128)(2,1)} %get-tuple-element.17.gr_in, ...), custom_call_target="tpu_custom_call" | custom-call | tf_op jit(solution)/shard_map/pallas_call | solution.py:505

commit v2 on v1

--- a/solution.py
+++ b/solution.py
@@ -101,29 +101,25 @@
             device_id={"dp": p}, device_id_type=pl.DeviceIdType.MESH,
         )
 
-    def send_kv(i, c):
-        dest = lax.rem(me + i, n)
-        in_copy(0, dest, me).start()
-        in_copy(1, dest, me).start()
-        return c
-
-    lax.fori_loop(1, n, send_kv, 0)
-    for a in range(4):
-        own_copy(a).start()
     my_group = me // group
 
-    def send_qg(t, c):
+    def partner(t):
+        value, bit = 0, 1
+        while bit < steps:
+            value = value + bit * lax.rem(my_group // bit + t // bit, 2)
+            bit *= 2
+        return value
+
+    def send_kv(t, c):
         for e in range(group):
-            dest = lax.rem(my_group + steps - t, steps) * group + e
+            dest = partner(t) * group + e
 
             @pl.when(dest != me)
             def _():
-                in_copy(2, dest, me).start()
-                in_copy(3, dest, me).start()
-
-        return c
-
-    lax.fori_loop(0, steps, send_qg, 0)
+                in_copy(0, dest, me).start()
+                in_copy(1, dest, me).start()
+
+        return c
 
     xf[...] = jnp.zeros_like(xf)
     xf[pl.ds(0, txt), :] = x_ref[...].astype(F32)
@@ -132,6 +128,21 @@
         xs[p] = whole_x[:, p * dloc:(p + 1) * dloc].astype(BF)
     for i in range(1, ndp):
         x_copy(lax.rem(dp + i, ndp), dp).start()
+    lax.fori_loop(0, steps, send_kv, 0)
+    for a in range(4):
+        own_copy(a).start()
+
+    def send_qg(t, c):
+        for e in range(group):
+            dest = partner(t) * group + e
+
+            @pl.when(dest != me)
+            def _():
+                in_copy(2, dest, me).start()
+                in_copy(3, dest, me).start()
+
+        return c
+
     xall[dp] = xs[dp]
     gf[...] = jnp.zeros_like(gf)
     gf[pl.ds(0, txt), :] = gt_ref[...].astype(F32)
@@ -163,27 +174,17 @@
     dkacc[...] = jnp.zeros_like(dkacc)
     dvacc[...] = jnp.zeros_like(dvacc)
 
-    def wait_kv(i, c):
-        source = lax.rem(me + i, n)
-        in_copy(0, me, source).wait_recv()
-        in_copy(1, me, source).wait_recv()
-        return c
-
-    lax.fori_loop(1, n, wait_kv, 0)
     for a in range(4):
         own_copy(a).wait()
-
-    lane_head = lax.broadcasted_iota(jnp.int32, (m, cols), 1) // HEAD_DIM
-
-    def build(r, c):
-        at = pl.ds(pl.multiple_of(r * 128, 128), 128)
-        lane = lax.broadcasted_iota(jnp.int32, (128, cols), 1)
-        row = lax.broadcasted_iota(jnp.int32, (128, cols), 0) + r * 128
+    def build(first, count):
+        at = pl.ds(first if isinstance(first, int) else pl.multiple_of(first, 128), count)
+        lane = lax.broadcasted_iota(jnp.int32, (count, cols), 1)
+        row = lax.broadcasted_iota(jnp.int32, (count, cols), 0) + first
         kk = kbuf[at, :]
         vv = vbuf[at, :]
         bias = jnp.where((row >= img + txt) & (lane == 0), -1e30, 0.0).astype(BF)
-        ones = jnp.ones((128, cols), BF)
-        zero = jnp.zeros((128, cols), BF)
+        ones = jnp.ones((count, cols), BF)
+        zero = jnp.zeros((count, cols), BF)
         kaug[at, :] = jnp.concatenate([kk, bias], axis=1)
         vaug[at, :] = jnp.concatenate([vv, ones], axis=1)
         for h in range(heads):
@@ -192,9 +193,23 @@
             vh[h, at, :] = jnp.concatenate(
                 [jnp.where(mine, vv, zero), jnp.where(mine, ones, zero)], axis=1
             )
-        return c
-
-    lax.fori_loop(0, length // 128, build, 0)
+
+    build(img, tkey)
+
+    def wait_kv(t, c):
+        for e in range(group):
+            source = partner(t) * group + e
+
+            @pl.when(source != me)
+            def _():
+                in_copy(0, me, source).wait_recv()
+                in_copy(1, me, source).wait_recv()
+
+            build(source * rows, rows)
+        return c
+
+    lax.fori_loop(0, steps, wait_kv, 0)
+    lax.fori_loop(0, steps, send_qg, 0)
     scale = 1.0 / math.sqrt(HEAD_DIM)
 
     def out_copy(a, dest, source):
@@ -211,18 +226,9 @@
         land = o_out if a == 0 else gr_out.at[a - 1]
         return pltpu.make_async_copy(at_rows(send, me), tile(land, me), loc_sem.at[5 + a])
 
-    def step(t, c):
-        which = lax.rem(my_group + t + steps - 1, steps)
-        first = jnp.where(t == 0, img, which * m)
-        for e in range(group):
-            source = which * group + e
-
-            @pl.when((t > 0) & (source != me))
-            def _():
-                in_copy(2, me, source).wait_recv()
-                in_copy(3, me, source).wait_recv()
-
-        at = pl.ds(pl.multiple_of(first, 128), m)
+    def attend(first, m):
+        at = pl.ds(first if isinstance(first, int) else pl.multiple_of(first, 128), m)
+        lane_head = lax.broadcasted_iota(jnp.int32, (m, cols), 1) // HEAD_DIM
         qs = qbuf[at, :] * jnp.asarray(scale, BF)
         g = gbuf[at, :].astype(F32)
         zero = jnp.zeros_like(qs)
@@ -251,24 +257,43 @@
             dq = dq + dotf(ds, kh[h])
         obuf[at, :] = ob
         dqbuf[at, :] = (dq * scale).astype(BF)
+
+    def accumulate(m):
+        stacked = pl.ds(0, heads * m)
+        dvacc[...] += dotf(pbuf[stacked, :], gst[stacked, :], TN)
+        dkacc[...] += dotf(sbuf[stacked, :], qst[stacked, :], TN)
+
+    attend(img, tkey)
+    accumulate(tkey)
+
+    def step(t, c):
+        which = partner(t)
+        for e in range(group):
+            source = which * group + e
+
+            @pl.when(source != me)
+            def _():
+                in_copy(2, me, source).wait_recv()
+                in_copy(3, me, source).wait_recv()
+
+        attend(which * m, m)
         for e in range(group):
             dest = which * group + e
 
-            @pl.when((t > 0) & (dest != me))
+            @pl.when(dest != me)
             def _():
                 out_copy(0, dest, me).start()
                 out_copy(1, dest, me).start()
 
-            @pl.when((t > 0) & (dest == me))
+            @pl.when(dest == me)
             def _():
                 own_out(0).start()
                 own_out(1).start()
 
-        dvacc[...] += dotf(pbuf[...], gst[...], TN)
-        dkacc[...] += dotf(sbuf[...], qst[...], TN)
-        return c
-
-    lax.fori_loop(0, steps + 1, step, 0)
+        accumulate(m)
+        return c
+
+    lax.fori_loop(0, steps, step, 0)
 
     text = pl.ds(img, tsub)
     tg[0] = dqbuf[text, :]
@@ -278,25 +303,27 @@
         t_copy(lax.rem(dp + i, ndp), dp).start()
     ot_out[...] = obuf[text, :].astype(F32)[:txt].astype(BF)
 
-    def send_dkv(i, c):
-        dest = lax.rem(me + i, n)
-        at = pl.ds(pl.multiple_of(dest * rows, 16), rows)
-        dkb[at, :] = dkacc[at, :].astype(BF)
-        dvb[at, :] = dvacc[at, :].astype(BF)
-
-        @pl.when(dest != me)
-        def _():
-            out_copy(2, dest, me).start()
-            out_copy(3, dest, me).start()
-
-        @pl.when(dest == me)
-        def _():
-            own_out(2).start()
-            own_out(3).start()
-
-        return c
-
-    lax.fori_loop(1, n + 1, send_dkv, 0)
+    def send_dkv(t, c):
+        for e in range(group):
+            dest = partner(t) * group + e
+            at = pl.ds(pl.multiple_of(dest * rows, 16), rows)
+            dkb[at, :] = dkacc[at, :].astype(BF)
+            dvb[at, :] = dvacc[at, :].astype(BF)
+
+            @pl.when(dest != me)
+            def _():
+                out_copy(2, dest, me).start()
+                out_copy(3, dest, me).start()
+
+            @pl.when(dest == me)
+            def _():
+                own_out(2).start()
+                own_out(3).start()
+
+        return c
+
+    near = QUAD // group
+    lax.fori_loop(near, steps, send_dkv, 0)
 
     tgl[dp] = tg[...]
     for i in range(1, ndp):
@@ -336,6 +363,7 @@
             dxs[b % QUAD, s * per + b // QUAD] = value[b * dblk:(b + 1) * dblk, :].astype(BF)
     for i in range(1, QUAD):
         d1_copy(lax.rem(part_of + i, QUAD), part_of).start()
+    lax.fori_loop(0, near, send_dkv, 0)
     x_out[...] = xall[...]
     tg_out[...] = tgl[...]
     for i in range(1, QUAD):
@@ -414,12 +442,12 @@
     for i in range(4):
         fetch(i).wait()
         put(i).start()
-        if i < 3:
-            value = dotf(x_ref[0], tg_ref[0, i], TN)
-            for s in range(1, x_ref.shape[0]):
-                value = value + dotf(x_ref[s], tg_ref[s, i], TN)
-            dwb[i] = value
-            put_dw(i).start()
+    for i in range(3):
+        value = dotf(x_ref[0], tg_ref[0, i], TN)
+        for s in range(1, x_ref.shape[0]):
+            value = value + dotf(x_ref[s], tg_ref[s, i], TN)
+        dwb[i] = value
+        put_dw(i).start()
     for i in range(4):
         put(i).wait()
     for j in range(3):
@@ -450,7 +478,8 @@
     vmem = pl.BlockSpec(memory_space=pltpu.VMEM)
     cfg = (n, ndp, rows, cols, txt, tsub, tkey, dloc, dblk, group)
     dma = pltpu.SemaphoreType.DMA
-    assert nb % QUAD == 0 and n % QUAD == 0
+    steps = n // group
+    assert nb % QUAD == 0 and n % QUAD == 0 and steps & (steps - 1) == 0
     o, gr, ot, dx, xa, tga = pl.pallas_call(
         functools.partial(kernel, cfg),
         out_shape=(

time: 125 us -> 123 us (0.984)
  Pallas kernels: 124 us -> 122 us
    pallas_call x1, Pallas kernels: 119 us -> 117 us  [local(): pl.pallas_call(functools.partial(kernel, cfg), out_shape=(jax.ShapeDtypeS...]
where the time goes in v2:
time: 123 us
  Pallas kernels  122 us (99%)
    pallas_call x1, Pallas kernels, local(): pl.pallas_call(functools.partial(kernel, cfg), out_shape=(jax.ShapeDtypeS...  117 us
    pallas_call x1, Pallas kernels, local(): pl.pallas_call(finish, out_shape=(jax.ShapeDtypeStruct(shape, BF), jax.Sh...  5.08 us

profile of v2, /device:TPU:7, one launch (start us, length us, event | category | flops | bytes accessed | tf_op | source)
XLA Modules:
  0.0 123.0 jit_solution(1856751961549512729)
XLA Ops:
  0.6 117.3 %shard_map.110 = (bf16[128,2048]{1,0:T(8,128)(2,1)}, bf16[3,128,2048]{2,1,0:T(8,128)(2,1)}, bf16[77,128]{1,0:T(8,128)(2,1)}, f32[152,77]{1,0:T(8,128)}, bf16[2,8...) custom-call(bf16[128,2048]{1,0:T(8,128)(2,1)} %bitcast.14, bf16[128,2048]{1,0:T(8,128)(2,1)} %bitcast.15, ...), custom_call_target="tpu_custom_call" | custom-call | tf_op jit(solution)/shard_map/pallas_call | solution.py:483
  117.9 5.1 %shard_map.111 = (bf16[128,2048]{1,0:T(8,128)(2,1)}, bf16[3,128,2048]{2,1,0:T(8,128)(2,1)}, bf16[77,128]{1,0:T(8,128)(2,1)}, f32[152,77]{1,0:T(8,128)}, f32[3,1216,128]{2,1,0:T(8,128)}) custom-call(bf16[128,2048]{1,0:T(8,128)(2,1)} %get-tuple-element.16.o_in, bf16[3,128,2048]{2,1,0:T(8,128)(2,1)} %get-tuple-element.17.gr_in, ...), custom_call_target="tpu_custom_call" | custom-call | tf_op jit(solution)/shard_map/pallas_call | solution.py:534
